TPU v7x, 32 devices: a whole 2x2x4 slice. The times are simulated.
32 devices in a mesh: row: 8 (over z, x), col: 4 (over y, core).
Axes of the slice: x: 2, y: 2, z: 4, core: 2. Of those that a mesh axis runs over, the one named last changes fastest.
Arguments:
- features: bfloat16 [14336, 2048], P('row', 'col'), may hold values from -6 to 6
- neighbours: int32 [14336, 32], P('row'), may hold values from -1 to 127, as said below
- node_valid: int32 [14336], P('row'), may hold values from 0 to 1, as said below
- weight_one: bfloat16 [2048, 2048], P(None, 'col'), may hold values from -0.125 to 0.125
- gamma_one: float32 [2048], P('col'), may hold values from 0.25 to 1.75
- beta_one: float32 [2048], P('col'), may hold values from -0.5 to 0.5
- weight_two: bfloat16 [2048, 2048], P(None, 'col'), may hold values from -0.125 to 0.125
- gamma_two: float32 [2048], P('col'), may hold values from 0.25 to 1.75
- beta_two: float32 [2048], P('col'), may hold values from -0.5 to 0.5
- cotangent: bfloat16 [14336, 2048], P('row', 'col'), may hold values from -6 to 6
Outputs:
- output: float32 [14336, 2048], P('row', 'col')
- grad_features: float32 [14336, 2048], P('row', 'col')
- grad_weight_one: float32 [2048, 2048], P(None, 'col')
- grad_gamma_one: float32 [2048], P('col')
- grad_beta_one: float32 [2048], P('col')
- grad_weight_two: float32 [2048, 2048], P(None, 'col')
- grad_gamma_two: float32 [2048], P('col')
- grad_beta_two: float32 [2048], P('col')
Inputs may be any that keep to these rules, and one draw needn't show every extreme that they name: `neighbours`: entries >= 0 name valid nodes of the same slot; every valid node has 1 to 32 such entries, first in its list, the rest are -1; a padding row has only -1; some slot is full. `node_valid`: in each slot the valid nodes come first and number at least 40.
All inputs are finite; a program needn't handle non-finite values.
Results may differ from a plain program's by a relative error of at most 0.012.
Values may be sent and summed in bfloat16 or wider, within the bound.
No kernel may reach another device: no remote copies, remote signals or barrier semaphores. Data moves between devices by JAX's collectives and lax.ppermute only.
A program may use at most 128 MiB of HBM per device.

v0:
```python
import jax
import jax.numpy as jnp
from jax import lax
from jax.sharding import PartitionSpec as P

SLOT = 128
NBR = 32
EPSILON = 1e-05


def build_tiles(neighbours):
    entries_all = neighbours.reshape(-1, SLOT, NBR)

    def build(entries):
        columns = jnp.arange(SLOT, dtype=jnp.int32)
        hits = jnp.sum((entries[:, :, None] == columns[None, None, :]).astype(jnp.float32), axis=1)
        degree = jnp.sum((entries >= 0).astype(jnp.float32), axis=1)
        joined = hits + jnp.eye(SLOT, dtype=jnp.float32)
        return joined / (degree[:, None] + 1.0)

    tiles = lax.map(build, entries_all)
    return (tiles, jnp.diagonal(tiles, axis1=1, axis2=2))


def spread(values, tiles, self_weight):
    shaped = values.reshape(tiles.shape[0], SLOT, values.shape[1])
    summed = jnp.einsum("sij,sjd->sid", tiles, shaped, precision=lax.Precision.HIGHEST)
    return (summed + self_weight[:, :, None] * shaped).reshape(values.shape)


def spread_back(grads, tiles, self_weight):
    shaped = grads.reshape(tiles.shape[0], SLOT, grads.shape[1])
    summed = jnp.einsum("sji,sjd->sid", tiles, shaped, precision=lax.Precision.HIGHEST)
    return (summed + self_weight[:, :, None] * shaped).reshape(grads.shape)


def moments(linear, valid):
    total_valid, summed = lax.psum((jnp.sum(valid), jnp.sum(valid * linear, axis=0)), "row")
    mean = summed / total_valid
    centred = linear - mean
    variance = lax.psum(jnp.sum(valid * centred * centred, axis=0), "row") / total_valid
    return (total_valid, mean, variance)


def forward_layer(values, weight, gamma, beta, tiles, self_weight, valid):
    mixed = spread(values, tiles, self_weight).astype(jnp.bfloat16)
    gathered = lax.all_gather(mixed, "col", axis=1, tiled=True)
    linear = jnp.dot(gathered, weight, preferred_element_type=jnp.float32)
    total_valid, mean, variance = moments(linear, valid)
    inv_std = lax.rsqrt(variance + EPSILON)
    normed = (linear - mean) * inv_std
    before = gamma * normed + beta
    result = valid * jax.nn.silu(before)
    return (result, (gathered, normed, inv_std, before, total_valid))


def backward_layer(grad_result, weight, gamma, kept, tiles, self_weight, valid):
    gathered, normed, inv_std, before, total_valid = kept
    sigmoid_value = jax.nn.sigmoid(before)
    slope = sigmoid_value * (1.0 + before * (1.0 - sigmoid_value))
    grad_before = grad_result * valid * slope
    grad_beta, grad_gamma = lax.psum(
        (jnp.sum(grad_before, axis=0), jnp.sum(grad_before * normed, axis=0)), "row"
    )
    grad_normed = gamma * grad_before
    grad_linear = inv_std * (
        grad_normed - valid * (gamma * grad_beta + normed * gamma * grad_gamma) / total_valid
    )
    grad_low = grad_linear.astype(jnp.bfloat16)
    weight_terms = lax.dot_general(
        gathered, grad_low, (((0,), (0,)), ((), ())), preferred_element_type=jnp.float32
    )
    grad_weight = lax.psum(weight_terms, "row")
    partial_terms = lax.dot_general(
        grad_low, weight, (((1,), (1,)), ((), ())), preferred_element_type=jnp.float32
    )
    grad_mixed = lax.psum_scatter(partial_terms, "col", scatter_dimension=1, tiled=True)
    grad_values = spread_back(grad_mixed, tiles, self_weight)
    return (grad_values, grad_weight, grad_gamma, grad_beta)


def local(
    features,
    neighbours,
    node_valid,
    weight_one,
    gamma_one,
    beta_one,
    weight_two,
    gamma_two,
    beta_two,
    cotangent,
):
    tiles, self_weight = build_tiles(neighbours)
    valid = node_valid.astype(jnp.float32)[:, None]
    hidden, kept_one = forward_layer(
        features.astype(jnp.float32), weight_one, gamma_one, beta_one, tiles, self_weight, valid
    )
    output, kept_two = forward_layer(
        hidden, weight_two, gamma_two, beta_two, tiles, self_weight, valid
    )
    grad_hidden, grad_weight_two, grad_gamma_two, grad_beta_two = backward_layer(
        cotangent.astype(jnp.float32), weight_two, gamma_two, kept_two, tiles, self_weight, valid
    )
    grad_features, grad_weight_one, grad_gamma_one, grad_beta_one = backward_layer(
        grad_hidden, weight_one, gamma_one, kept_one, tiles, self_weight, valid
    )
    return (
        output,
        grad_features,
        grad_weight_one,
        grad_gamma_one,
        grad_beta_one,
        grad_weight_two,
        grad_gamma_two,
        grad_beta_two,
    )


def solution(mesh):
    placed = (
        P("row", "col"),
        P("row", None),
        P("row"),
        P(None, "col"),
        P("col"),
        P("col"),
        P(None, "col"),
        P("col"),
        P("col"),
        P("row", "col"),
    )
    return jax.shard_map(
        local,
        mesh=mesh,
        in_specs=placed,
        out_specs=(
            P("row", "col"),
            P("row", "col"),
            P(None, "col"),
            P("col"),
            P("col"),
            P(None, "col"),
            P("col"),
            P("col"),
        ),
        check_vma=False,
    )
```

profile of v0, /device:TPU:0, one launch (start us, length us, event | category | flops | bytes accessed | tf_op | source)
XLA Modules:
  0.0 855.5 jit_solution(2408295498759646820)
XLA Ops:
  9.6 27.6 %while.10 = (s32[]{:T(128)}, f32[14,128,128]{2,1,0:T(8,128)S(1)}, s32[14,128,32]{2,1,0:T(8,128)}, s32[]{:T(128)}) while((s32[]{:T(128)}, f32[14,128,128]{2,1,0:T(8,128)S(1)}, s32[14,128,32]{2,1,0:T(8,128)}, s32[]{:T(128)}) %tuple.47), condition=%wide.region_3.4_spmd, body=%wide.region_0.3_spmd.sunk | while | flops 1634306 | bytes 247877 | solution.py:21
  43.7 5.1 add_convert_fusion.1
  49.5 54.5 %all-gather.3.cloned.1.call-done = bf16[1792,2048]{1,0:T(8,128)(2,1)} async-done(((bf16[1792,512]{1,0:T(8,128)(2,1)}), bf16[1792,2048]{1,0:T(8,128)(2,1)}) %all-gather.3.cloned.1.call-update) | async-done | bytes 7340048 | tf_op jit(solution)/shard_map/all_gather | solution.py:47
  104.0 9.5 %multiply_reduce_fusion.3 = (f32[512]{0:T(512)S(1)}, f32[1792,512]{1,0:T(8,128)}) fusion(f32[1792]{0:T(1024)S(1)} %convert_element_type.41, bf16[1792,2048]{1,0:T(8,128)(2,1)} %all-gather.3.cloned.1.call-done, bf16[2048,512]{1,0:T(8,128)(2,1)} %param.15), kind=kOutput, calls=%fused_computation.29 | convolution fusion | flops 3759930880 | bytes 13116416 | tf_op jit(solution)/shard_map/dot_general | solution.py:48
  113.5 22.0 %all-reduce.2 = (f32[512]{0:T(512)S(1)}, f32[]{:T(128)}) all-reduce(f32[512]{0:T(512)S(1)} %get-tuple-element.49, f32[]{:T(128)} %convert_reduce_fusion.2), channel_id=1, replica_groups=mesh['row'=8,'col'=4] {'row'}, use_global_device_ids=true, to_apply=%region_5.6 | all-reduce | flops 513 | bytes 4104 | tf_op jit(solution)/shard_map/psum | solution.py:38
  138.6 17.1 %psum.82 = f32[512]{0:T(512)S(1)} all-reduce(f32[512]{0:T(512)S(1)} %fusion.2), channel_id=1, replica_groups=mesh['row'=8,'col'=4] {'row'}, use_global_device_ids=true, to_apply=%region_9.10 | all-reduce | flops 512 | bytes 4096 | tf_op jit(solution)/shard_map/psum | solution.py:41
  164.1 50.0 %all-gather.5.cloned.1.call-done = bf16[1792,2048]{1,0:T(8,128)(2,1)} async-done(((bf16[1792,512]{1,0:T(8,128)(2,1)}), bf16[1792,2048]{1,0:T(8,128)(2,1)}) %all-gather.5.cloned.1.call-update) | async-done | bytes 7340048 | tf_op jit(solution)/shard_map/all_gather | solution.py:47
  214.1 8.9 %multiply_reduce_fusion.2 = (f32[512]{0:T(512)S(1)}, f32[1792,512]{1,0:T(8,128)}) fusion(f32[1792]{0:T(1024)S(1)} %convert_element_type.41, bf16[1792,2048]{1,0:T(8,128)(2,1)} %all-gather.5.cloned.1.call-done, bf16[2048,512]{1,0:T(8,128)(2,1)S(1)} %copy-done), kind=kOutput, calls=%fused_computation.25 | convolution fusion | flops 3759930880 | bytes 13116416 | tf_op jit(solution)/shard_map/dot_general | solution.py:48
  223.0 21.5 %psum.83 = f32[512]{0:T(512)S(1)} all-reduce(f32[512]{0:T(512)S(1)} %get-tuple-element.51), channel_id=1, replica_groups=mesh['row'=8,'col'=4] {'row'}, use_global_device_ids=true, to_apply=%region_11.12 | all-reduce | flops 512 | bytes 4096 | tf_op jit(solution)/shard_map/psum | solution.py:38
  247.7 17.1 %psum.84 = f32[512]{0:T(512)S(1)} all-reduce(f32[512]{0:T(512)S(1)} %fusion.3), channel_id=1, replica_groups=mesh['row'=8,'col'=4] {'row'}, use_global_device_ids=true, to_apply=%region_13.14 | all-reduce | flops 512 | bytes 4096 | tf_op jit(solution)/shard_map/psum | solution.py:41
  265.4 6.3 fusion.6
  271.7 19.1 %all-reduce.1 = (f32[512]{0:T(512)S(1)}, f32[512]{0:T(512)S(1)}) all-reduce(f32[512]{0:T(512)S(1)} %get-tuple-element.29, f32[512]{0:T(512)S(1)} %get-tuple-element.28), channel_id=1, replica_groups=mesh['row'=8,'col'=4] {'row'}, use_global_device_ids=true, to_apply=%region_17.18 | all-reduce | flops 1024 | bytes 8192 | tf_op jit(solution)/shard_map/psum | solution.py:62
  296.6 7.2 fusion.8
  304.1 109.0 %reduce-scatter.3.cloned.1.call-done = f32[1792,512]{1,0:T(8,128)} async-done(((f32[1792,2048]{1,0:T(8,128)}), f32[1792,512]{1,0:T(8,128)}) %reduce-scatter.3.cloned.1.call-update) | async-done | bytes 3670032 | tf_op jit(solution)/shard_map/reduce_scatter | solution.py:77
  413.1 6.8 multiply_add_fusion.1
  423.7 21.3 %all-reduce = (f32[512]{0:T(512)S(1)}, f32[512]{0:T(512)S(1)}) all-reduce(f32[512]{0:T(512)S(1)} %get-tuple-element.27, f32[512]{0:T(512)S(1)} %get-tuple-element.26), channel_id=1, replica_groups=mesh['row'=8,'col'=4] {'row'}, use_global_device_ids=true, to_apply=%region_22.23 | all-reduce | flops 1024 | bytes 8192 | tf_op jit(solution)/shard_map/psum | solution.py:62
  445.0 4.7 multiply_convert_fusion
  449.8 7.3 fusion.9
  458.5 9.9 %fusion.11 = f32[2048,512]{1,0:T(8,128)} fusion(bf16[1792,2048]{1,0:T(8,128)(2,1)} %all-gather.5.cloned.1.call-done, bf16[1792,512]{1,0:T(8,128)(2,1)S(1)} %copy-done.5), kind=kOutput, calls=%fused_computation.44 | convolution fusion | flops 3758096384 | bytes 13369344 | tf_op jit(solution)/shard_map/dot_general | solution.py:70
  468.4 10.5 %fusion.10 = f32[2048,512]{1,0:T(8,128)} fusion(bf16[1792,2048]{1,0:T(8,128)(2,1)} %all-gather.3.cloned.1.call-done, bf16[1792,512]{1,0:T(8,128)(2,1)S(1)} %copy-done.7), kind=kOutput, calls=%fused_computation.43 | convolution fusion | flops 3758096384 | bytes 13369344 | tf_op jit(solution)/shard_map/dot_general | solution.py:70
  479.0 87.5 %reduce-scatter.5.cloned.1.call-done = f32[1792,512]{1,0:T(8,128)} async-done(((f32[1792,2048]{1,0:T(8,128)}), f32[1792,512]{1,0:T(8,128)}) %reduce-scatter.5.cloned.1.call-update) | async-done | bytes 3670032 | tf_op jit(solution)/shard_map/reduce_scatter | solution.py:77
  566.5 8.5 multiply_add_fusion
  575.0 267.1 %all-reduce.6.cloned.1.call-done = (f32[2048,512]{1,0:T(8,128)}, f32[2048,512]{1,0:T(8,128)}) async-done(((f32[2048,512]{1,0:T(8,128)}, f32[2048,512]{1,0:T(8,128)}), (f32[2048,512]{1,0:T(8,128)}, f32[2048,512]{1,0:T(8,128)})) %all-reduce.6.cloned.1.call-update) | async-done | bytes 8388624 | tf_op jit(solution)/shard_map/psum | solution.py:73
  842.1 4.8 copy.41
  (123 shorter events, 65.0 us)
Async XLA Ops:
  7.2 207.0 %copy-start = (bf16[2048,512]{1,0:T(8,128)(2,1)S(1)}, bf16[2048,512]{1,0:T(8,128)(2,1)}, u32[]{:S(2)}) copy-start(bf16[2048,512]{1,0:T(8,128)(2,1)} %param.18) | copy-start | bytes 6291460
  7.2 96.8 %all-gather.3.cloned.1.call-start = ((), (), s32[]{:S(2)}) async-start(), calls=%async_computation.2 | async-start | bytes 9175040 | tf_op jit(solution)/shard_map/all_gather | solution.py:47
  41.8 7.0 copy-start.8
  48.8 165.3 %all-gather.5.cloned.1.call-start = ((), (), s32[]{:S(2)}) async-start(), calls=%async_computation.3 | async-start | bytes 9175040 | tf_op jit(solution)/shard_map/all_gather | solution.py:47
  113.5 42.8 %copy-start.9 = (f32[512]{0:T(512)S(1)}, f32[512]{0:T(512)}, u32[]{:S(2)}) copy-start(f32[512]{0:T(512)} %param.16) | copy-start | bytes 6148
  113.5 42.8 %copy-start.11 = (f32[512]{0:T(512)S(1)}, f32[512]{0:T(512)}, u32[]{:S(2)}) copy-start(f32[512]{0:T(512)} %param.17) | copy-start | bytes 6148
  163.9 249.3 %reduce-scatter.3.cloned.1.call-start = ((), (), s32[]{:S(2)}) async-start(), calls=%async_computation.4 | async-start | bytes 18350080 | tf_op jit(solution)/shard_map/reduce_scatter | solution.py:77
  223.0 42.3 %copy-start.10 = (f32[512]{0:T(512)S(1)}, f32[512]{0:T(512)}, u32[]{:S(2)}) copy-start(f32[512]{0:T(512)} %param.19) | copy-start | bytes 6148
  223.0 42.3 %copy-start.12 = (f32[512]{0:T(512)S(1)}, f32[512]{0:T(512)}, u32[]{:S(2)}) copy-start(f32[512]{0:T(512)} %param.20) | copy-start | bytes 6148
  290.8 4.5 copy-start.13
  290.8 4.6 copy-start.15
  295.3 1.2 copy-start.4
  303.8 262.6 %reduce-scatter.5.cloned.1.call-start = ((), (), s32[]{:S(2)}) async-start(), calls=%async_computation.5 | async-start | bytes 18350080 | tf_op jit(solution)/shard_map/reduce_scatter | solution.py:77
  413.1 6.8 copy-start.2
  445.0 4.7 copy-start.14
  445.0 4.7 copy-start.16
  445.0 4.7 copy-start.17
  449.7 7.3 copy-start.6
  457.0 1.5 copy-start.5
  457.0 385.1 %all-reduce.6.cloned.1.call-start = ((), (), s32[]{:S(2)}) async-start(), calls=%async_computation.6 | async-start | bytes 16777216 | tf_op jit(solution)/shard_map/psum | solution.py:73
  458.5 9.9 %copy-start.7 = (bf16[1792,512]{1,0:T(8,128)(2,1)S(1)}, bf16[1792,512]{1,0:T(8,128)(2,1)}, u32[]{:S(2)}) copy-start(bf16[1792,512]{1,0:T(8,128)(2,1)} %copy-done.6) | copy-start | bytes 5505028
  842.1 4.8 copy-start.3
  842.1 6.8 copy-start.1
Sparse Core Ops, SparseCore 0:
  48.9 55.0 all-gather.2
  164.0 50.1 all-gather.4
  303.9 109.1 reduce-scatter.2
  457.2 109.2 reduce-scatter.4
  571.0 271.0 all-reduce.5
where the time goes:
time: 857 us; the launch traced here: 855 us
  waiting for transfers between devices  568 us (66%)
  blocking collectives  118 us (14%)
  matrix products  78.2 us (9%)
  other arithmetic  57.2 us (7%)
  local copies, waits for them, and re-layouts  18.1 us (2%)
  between operations  14 us (2%)
    psum x1, waiting for transfers between devices, backward_layer(): grad_weight = lax.psum(weight_terms, 'row')  267 us
    reduce_scatter x2, waiting for transfers between devices, backward_layer(): lax.psum_scatter(partial_terms, 'col', scatter_dimension=1, tiled=True)  197 us
    all_gather x2, waiting for transfers between devices, forward_layer(): gathered = lax.all_gather(mixed, 'col', axis=1, tiled=True)  105 us
    psum x2, blocking collectives, moments(): lax.psum((jnp.sum(valid), jnp.sum(valid * linear, axis=0)), 'row')  43.4 us
    psum x2, blocking collectives, backward_layer(): lax.psum((jnp.sum(grad_before, axis=0), jnp.sum(grad_before * normed, axi...  40.5 us
    psum x2, blocking collectives, moments(): lax.psum(jnp.sum(valid * centred * centred, axis=0), 'row') / total_valid  34.3 us
    dot_general x2, matrix products, backward_layer(): lax.dot_general(gathered, grad_low, (((0,), (0,)), ((), ())), preferred_e...  20.4 us
    dot_general x2, matrix products, forward_layer(): linear = jnp.dot(gathered, weight, preferred_element_type=jnp.float32)  18.4 us
  transfers between devices with their start and end apart: 5, of which 5 were waited for; matrix products, arithmetic and copies ran while one was open for 3% of the time, Pallas kernels for 0%

commit v1 on v0

--- a/solution.py
+++ b/solution.py
@@ -44,7 +44,14 @@
 
 def forward_layer(values, weight, gamma, beta, tiles, self_weight, valid):
     mixed = spread(values, tiles, self_weight).astype(jnp.bfloat16)
-    gathered = lax.all_gather(mixed, "col", axis=1, tiled=True)
+    ways, here, step = (lax.axis_size("col"), lax.axis_index("col"), mixed.shape[1])
+    line, have = (mixed, 1)
+    while have < ways:
+        line = jnp.concatenate(
+            [line, lax.ppermute(line, "col", [(d, (d - have) % ways) for d in range(ways)])], axis=1
+        )
+        have = 2 * have
+    gathered = jnp.roll(line, here * step, axis=1)
     linear = jnp.dot(gathered, weight, preferred_element_type=jnp.float32)
     total_valid, mean, variance = moments(linear, valid)
     inv_std = lax.rsqrt(variance + EPSILON)

time: 857 us -> 977 us (1.14)
  waiting for transfers between devices: 568 us -> 668 us
  other arithmetic: 57.2 us -> 77.2 us
    ppermute x0 -> x4, waiting for transfers between devices: none -> 204 us  [forward_layer(): lax.ppermute(line, 'col', [(d, (d - have) % ways) for d in range(ways)])]
    all_gather x2 -> x0, waiting for transfers between devices: 105 us -> none  [forward_layer(): gathered = lax.all_gather(mixed, 'col', axis=1, tiled=True)]
    concatenate x0 -> x4, other arithmetic: none -> 19.9 us  [the longest x2 16.9 us: forward_layer(): gathered = jnp.roll(line, here * step, axis=1)]
  transfers between devices with their start and end apart: 5 -> 7, of which waited for: 5 -> 7; matrix products, arithmetic and copies ran while one was open for 3% -> 3% of each run, Pallas kernels for 0% -> 0%
where the time goes in v1:
time: 977 us; the launch traced here: 969 us
  waiting for transfers between devices  668 us (68%)
  blocking collectives  117 us (12%)
  other arithmetic  77.2 us (8%)
  matrix products  69.6 us (7%)
  local copies, waits for them, and re-layouts  18.2 us (2%)
  between operations  14.3 us (1%)
    psum x1, waiting for transfers between devices, backward_layer(): grad_weight = lax.psum(weight_terms, 'row')  267 us
    ppermute x4, waiting for transfers between devices, forward_layer(): lax.ppermute(line, 'col', [(d, (d - have) % ways) for d in range(ways)])  204 us
    reduce_scatter x2, waiting for transfers between devices, backward_layer(): lax.psum_scatter(partial_terms, 'col', scatter_dimension=1, tiled=True)  196 us
    psum x2, blocking collectives, moments(): lax.psum((jnp.sum(valid), jnp.sum(valid * linear, axis=0)), 'row')  41.5 us
    psum x2, blocking collectives, backward_layer(): lax.psum((jnp.sum(grad_before, axis=0), jnp.sum(grad_before * normed, axi...  40.6 us
    psum x2, blocking collectives, moments(): lax.psum(jnp.sum(valid * centred * centred, axis=0), 'row') / total_valid  34.7 us
    dot_general x2, matrix products, backward_layer(): lax.dot_general(gathered, grad_low, (((0,), (0,)), ((), ())), preferred_e...  20.4 us
  transfers between devices with their start and end apart: 7, of which 7 were waited for; matrix products, arithmetic and copies ran while one was open for 3% of the time, Pallas kernels for 0%

profile of v1, /device:TPU:0, one launch (start us, length us, event | category | flops | bytes accessed | tf_op | source)
XLA Modules:
  0.0 968.6 jit_solution(12378213569797727600)
XLA Ops:
  9.6 27.6 %while.10 = (s32[]{:T(128)}, f32[14,128,128]{2,1,0:T(8,128)S(1)}, s32[14,128,32]{2,1,0:T(8,128)}, s32[]{:T(128)}) while((s32[]{:T(128)}, f32[14,128,128]{2,1,0:T(8,128)S(1)}, s32[14,128,32]{2,1,0:T(8,128)}, s32[]{:T(128)}) %tuple.44), condition=%wide.region_3.4_spmd, body=%wide.region_0.3_spmd.sunk | while | flops 1634306 | bytes 247877 | solution.py:21
  50.0 20.7 %collective-permute-done = bf16[1792,512]{1,0:T(8,128)(2,1)S(1)} collective-permute-done((bf16[1792,512]{1,0:T(8,128)(2,1)S(1)}, bf16[1792,512]{1,0:T(8,128)(2,1)S(1)}, u32[]{:S(2)}, u32[]{:S(2)}) %collective-permute-start) | collective-permute-done | bytes 1835040 | tf_op jit(solution)/shard_map/ppermute | solution.py:51
  74.4 81.2 %collective-permute-done.1 = bf16[1792,1024]{1,0:T(8,128)(2,1)} collective-permute-done((bf16[1792,1024]{1,0:T(8,128)(2,1)}, bf16[1792,1024]{1,0:T(8,128)(2,1)}, u32[]{:S(2)}, u32[]{:S(2)}) %collective-permute-start.1) | collective-permute-done | bytes 3670048 | tf_op jit(solution)/shard_map/ppermute | solution.py:51
  155.6 9.8 %fusion.9 = bf16[1792,2048]{1,0:T(8,128)(2,1)S(1)} fusion(s32[]{:T(128)S(6)} %select_n.17, bf16[1792,512]{1,0:T(8,128)(2,1)} %bitcast.49, bf16[1792,512]{1,0:T(8,128)(2,1)} %copy-done.6, bf16[1792,1024]{1,0:T(8,128)(2,1)} %collective-permute-done.1), kind=kLoop, calls=%fused_computation.29 | loop fusion | flops 44040192 | bytes 14680068 | tf_op jit(solution)/shard_map/jit(_roll_dynamic)/concatenate | solution.py:54
  171.4 22.3 %all-reduce.2 = (f32[512]{0:T(512)S(1)}, f32[]{:T(128)}) all-reduce(f32[512]{0:T(512)S(1)} %get-tuple-element.50, f32[]{:T(128)} %convert_reduce_fusion.2), channel_id=1, replica_groups=mesh['row'=8,'col'=4] {'row'}, use_global_device_ids=true, to_apply=%region_5.7 | all-reduce | flops 513 | bytes 4104 | tf_op jit(solution)/shard_map/psum | solution.py:38
  196.8 17.6 %psum.82 = f32[512]{0:T(512)S(1)} all-reduce(f32[512]{0:T(512)S(1)} %fusion.12), channel_id=1, replica_groups=mesh['row'=8,'col'=4] {'row'}, use_global_device_ids=true, to_apply=%region_9.11 | all-reduce | flops 512 | bytes 4096 | tf_op jit(solution)/shard_map/psum | solution.py:41
  221.9 20.7 %collective-permute-done.2 = bf16[1792,512]{1,0:T(8,128)(2,1)S(1)} collective-permute-done((bf16[1792,512]{1,0:T(8,128)(2,1)S(1)}, bf16[1792,512]{1,0:T(8,128)(2,1)S(1)}, u32[]{:S(2)}, u32[]{:S(2)}) %collective-permute-start.2) | collective-permute-done | bytes 1835040 | tf_op jit(solution)/shard_map/ppermute | solution.py:51
  243.3 81.8 %collective-permute-done.3 = bf16[1792,1024]{1,0:T(8,128)(2,1)S(1)} collective-permute-done((bf16[1792,1024]{1,0:T(8,128)(2,1)S(1)}, bf16[1792,1024]{1,0:T(8,128)(2,1)S(1)}, u32[]{:S(2)}, u32[]{:S(2)}) %collective-permute-start.3) | collective-permute-done | bytes 3670048 | tf_op jit(solution)/shard_map/ppermute | solution.py:51
  325.1 7.1 fusion.4
  332.2 5.9 multiply_reduce_fusion.2
  338.1 19.3 %psum.83 = f32[512]{0:T(512)S(1)} all-reduce(f32[512]{0:T(512)S(1)} %get-tuple-element.52), channel_id=1, replica_groups=mesh['row'=8,'col'=4] {'row'}, use_global_device_ids=true, to_apply=%region_11.13 | all-reduce | flops 512 | bytes 4096 | tf_op jit(solution)/shard_map/psum | solution.py:38
  360.5 17.1 %psum.84 = f32[512]{0:T(512)S(1)} all-reduce(f32[512]{0:T(512)S(1)} %fusion.13), channel_id=1, replica_groups=mesh['row'=8,'col'=4] {'row'}, use_global_device_ids=true, to_apply=%region_13.15 | all-reduce | flops 512 | bytes 4096 | tf_op jit(solution)/shard_map/psum | solution.py:41
  378.3 6.3 fusion.16
  384.5 19.3 %all-reduce.1 = (f32[512]{0:T(512)S(1)}, f32[512]{0:T(512)S(1)}) all-reduce(f32[512]{0:T(512)S(1)} %get-tuple-element.30, f32[512]{0:T(512)S(1)} %get-tuple-element.29), channel_id=1, replica_groups=mesh['row'=8,'col'=4] {'row'}, use_global_device_ids=true, to_apply=%region_17.19 | all-reduce | flops 1024 | bytes 8192 | tf_op jit(solution)/shard_map/psum | solution.py:69
  409.6 7.2 fusion.18
  416.9 108.9 %reduce-scatter.3.cloned.1.call-done = f32[1792,512]{1,0:T(8,128)} async-done(((f32[1792,2048]{1,0:T(8,128)}), f32[1792,512]{1,0:T(8,128)}) %reduce-scatter.3.cloned.1.call-update) | async-done | bytes 3670032 | tf_op jit(solution)/shard_map/reduce_scatter | solution.py:84
  525.8 6.8 multiply_add_fusion.1
  536.4 21.3 %all-reduce = (f32[512]{0:T(512)S(1)}, f32[512]{0:T(512)S(1)}) all-reduce(f32[512]{0:T(512)S(1)} %get-tuple-element.28, f32[512]{0:T(512)S(1)} %get-tuple-element.27), channel_id=1, replica_groups=mesh['row'=8,'col'=4] {'row'}, use_global_device_ids=true, to_apply=%region_22.24 | all-reduce | flops 1024 | bytes 8192 | tf_op jit(solution)/shard_map/psum | solution.py:69
  562.5 7.3 fusion.19
  571.2 9.9 %fusion.21 = f32[2048,512]{1,0:T(8,128)} fusion(bf16[1792,2048]{1,0:T(8,128)(2,1)} %copy-done.5, bf16[1792,512]{1,0:T(8,128)(2,1)S(1)} %copy-done.9), kind=kOutput, calls=%fused_computation.68 | convolution fusion | flops 3758096384 | bytes 13369344 | tf_op jit(solution)/shard_map/dot_general | solution.py:77
  581.1 10.5 %fusion.20 = f32[2048,512]{1,0:T(8,128)} fusion(bf16[1792,2048]{1,0:T(8,128)(2,1)} %copy-done.4, bf16[1792,512]{1,0:T(8,128)(2,1)S(1)} %copy-done.11), kind=kOutput, calls=%fused_computation.67 | convolution fusion | flops 3758096384 | bytes 13369344 | tf_op jit(solution)/shard_map/dot_general | solution.py:77
  591.6 87.6 %reduce-scatter.5.cloned.1.call-done = f32[1792,512]{1,0:T(8,128)} async-done(((f32[1792,2048]{1,0:T(8,128)}), f32[1792,512]{1,0:T(8,128)}) %reduce-scatter.5.cloned.1.call-update) | async-done | bytes 3670032 | tf_op jit(solution)/shard_map/reduce_scatter | solution.py:84
  679.2 8.5 multiply_add_fusion
  687.7 267.3 %all-reduce.6.cloned.1.call-done = (f32[2048,512]{1,0:T(8,128)}, f32[2048,512]{1,0:T(8,128)}) async-done(((f32[2048,512]{1,0:T(8,128)}, f32[2048,512]{1,0:T(8,128)}), (f32[2048,512]{1,0:T(8,128)}, f32[2048,512]{1,0:T(8,128)})) %all-reduce.6.cloned.1.call-update) | async-done | bytes 8388624 | tf_op jit(solution)/shard_map/psum | solution.py:80
  (139 shorter events, 89.2 us)
Async XLA Ops:
  7.2 325.0 %copy-start = (bf16[2048,512]{1,0:T(8,128)(2,1)S(1)}, bf16[2048,512]{1,0:T(8,128)(2,1)}, u32[]{:S(2)}) copy-start(bf16[2048,512]{1,0:T(8,128)(2,1)} %param.20) | copy-start | bytes 6291460
  7.2 518.6 %reduce-scatter.3.cloned.1.call-start = ((), (), s32[]{:S(2)}) async-start(), calls=%async_computation.2 | async-start | bytes 18350080 | tf_op jit(solution)/shard_map/reduce_scatter | solution.py:84
  47.6 25.7 %copy-start.3 = (bf16[14,128,512]{2,1,0:T(8,128)(2,1)}, bf16[14,128,512]{2,1,0:T(8,128)(2,1)S(1)}, u32[]{:S(2)}) copy-start(bf16[14,128,512]{2,1,0:T(8,128)(2,1)S(1)} %add_convert_fusion.1) | copy-start | bytes 5505028
  47.6 26.2 %copy-start.12 = (s32[1792]{0:T(1024)S(1)}, s32[1792]{0:T(1024)}, u32[]{:S(2)}) copy-start(s32[1792]{0:T(1024)} %param.16) | copy-start | bytes 21508
  47.6 23.2 %collective-permute-start = (bf16[1792,512]{1,0:T(8,128)(2,1)S(1)}, bf16[1792,512]{1,0:T(8,128)(2,1)S(1)}, u32[]{:S(2)}, u32[]{:S(2)}) collective-permute-start(bf16[1792,512]{1,0:T(8,128)(2,1)S(1)} %bitcast.47), channel_id=1, source_target_pairs={{0,3},{1,0},{2,1},{3,2},{4,7},{5,4},{6,5},{7,6},{8,11},{9,8},{10,9... | collective-permute-start | bytes 5505032 | tf_op jit(solution)/shard_map/ppermute | solution.py:51
  73.2 82.4 %collective-permute-start.1 = (bf16[1792,1024]{1,0:T(8,128)(2,1)}, bf16[1792,1024]{1,0:T(8,128)(2,1)}, u32[]{:S(2)}, u32[]{:S(2)}) collective-permute-start(bf16[1792,1024]{1,0:T(8,128)(2,1)} %pad_maximum_fusion), channel_id=1, source_target_pairs={{0,2},{1,3},{2,0},{3,1},{4,6},{5,7},{6,4},{7,5},{8,10},{9,11},{10,... | collective-permute-start | bytes 11010056 | tf_op jit(solution)/shard_map/ppermute | solution.py:51
  74.4 91.1 %copy-start.21 = (bf16[2048,512]{1,0:T(8,128)(2,1)S(1)}, bf16[2048,512]{1,0:T(8,128)(2,1)}, u32[]{:S(2)}) copy-start(bf16[2048,512]{1,0:T(8,128)(2,1)} %param.17) | copy-start | bytes 6291460
  165.5 5.9 copy-start.4
  171.4 43.6 %copy-start.13 = (f32[512]{0:T(512)S(1)}, f32[512]{0:T(512)}, u32[]{:S(2)}) copy-start(f32[512]{0:T(512)} %param.18) | copy-start | bytes 6148
  171.4 43.6 %copy-start.15 = (f32[512]{0:T(512)S(1)}, f32[512]{0:T(512)}, u32[]{:S(2)}) copy-start(f32[512]{0:T(512)} %param.19) | copy-start | bytes 6148
  221.8 20.8 %collective-permute-start.2 = (bf16[1792,512]{1,0:T(8,128)(2,1)S(1)}, bf16[1792,512]{1,0:T(8,128)(2,1)S(1)}, u32[]{:S(2)}, u32[]{:S(2)}) collective-permute-start(bf16[1792,512]{1,0:T(8,128)(2,1)S(1)} %bitcast.50), channel_id=1, source_target_pairs={{0,3},{1,0},{2,1},{3,2},{4,7},{5,4},{6,5},{7,6},{8,11},{9,8},{10,9... | collective-permute-start | bytes 5505032 | tf_op jit(solution)/shard_map/ppermute | solution.py:51
  243.2 81.9 %collective-permute-start.3 = (bf16[1792,1024]{1,0:T(8,128)(2,1)S(1)}, bf16[1792,1024]{1,0:T(8,128)(2,1)S(1)}, u32[]{:S(2)}, u32[]{:S(2)}) collective-permute-start(bf16[1792,1024]{1,0:T(8,128)(2,1)S(1)} %pad_maximum_fusion.1), channel_id=1, source_target_pairs={{0,2},{1,3},{2,0},{3,1},{4,6},{5,7},{6,4},{7,5},{8,10},{9,11},{10,... | collective-permute-start | bytes 11010056 | tf_op jit(solution)/shard_map/ppermute | solution.py:51
  332.2 5.9 copy-start.5
  338.1 40.1 %copy-start.14 = (f32[512]{0:T(512)S(1)}, f32[512]{0:T(512)}, u32[]{:S(2)}) copy-start(f32[512]{0:T(512)} %param.21) | copy-start | bytes 6148
  338.1 40.1 %copy-start.16 = (f32[512]{0:T(512)S(1)}, f32[512]{0:T(512)}, u32[]{:S(2)}) copy-start(f32[512]{0:T(512)} %param.22) | copy-start | bytes 6148
  416.9 262.3 %reduce-scatter.5.cloned.1.call-start = ((), (), s32[]{:S(2)}) async-start(), calls=%async_computation.3 | async-start | bytes 18350080 | tf_op jit(solution)/shard_map/reduce_scatter | solution.py:84
  525.8 6.8 copy-start.2
  557.7 4.7 copy-start.20
  557.7 4.7 copy-start.22
  562.4 7.3 copy-start.10
  569.7 385.2 %all-reduce.6.cloned.1.call-start = ((), (), s32[]{:S(2)}) async-start(), calls=%async_computation.4 | async-start | bytes 16777216 | tf_op jit(solution)/shard_map/psum | solution.py:80
  571.2 9.9 %copy-start.11 = (bf16[1792,512]{1,0:T(8,128)(2,1)S(1)}, bf16[1792,512]{1,0:T(8,128)(2,1)}, u32[]{:S(2)}) copy-start(bf16[1792,512]{1,0:T(8,128)(2,1)} %copy-done.10) | copy-start | bytes 5505028
  955.0 4.8 copy-start.7
  955.0 6.8 copy-start.1
  (6 other events, 19.0 us)
Sparse Core Ops, SparseCore 0:
  417.0 108.7 reduce-scatter.2
  569.9 109.2 reduce-scatter.4
  683.8 271.1 all-reduce.5
